TPU v7x, 256 devices: a whole 4x4x8 slice. The times are simulated.
256 devices in a mesh: dom: 8 (over y, core), shard: 32 (over x, z).
Axes of the slice: x: 4, y: 4, z: 8, core: 2. Of those that a mesh axis runs over, the one named last changes fastest.
Arguments:
- features: bfloat16 [65536, 512], P(('dom', 'shard')), may hold values from -6 to 6
- w_self: bfloat16 [512, 512], replicated, may hold values from -0.25 to 0.25
- w_neigh: bfloat16 [512, 512], replicated, may hold values from -0.25 to 0.25
- cotangent: bfloat16 [65536, 512], P(('dom', 'shard')), may hold values from -6 to 6
- neighbours: int32 [65536, 32], P(('dom', 'shard')), may hold values from 0 to 640, as said below
- hub_slots: int32 [256], P(('dom', 'shard')), may hold values from 0 to 255, as said below
- send_rows: int32 [256, 32, 4], P(('dom', 'shard')), may hold values from 0 to 255, as said below
- send_counts: int32 [256, 32], P(('dom', 'shard')), may hold values from 1 to 4, as said below
Outputs:
- hidden: bfloat16 [65536, 512], P(('dom', 'shard'))
- grad_features: float32 [65536, 512], P(('dom', 'shard'))
- grad_self: float32 [512, 512], replicated
- grad_neigh: float32 [512, 512], replicated
Inputs may be any that keep to these rules, and one draw needn't show every extreme that they name: `neighbours`: padding slots (640) come after a vertex's live slots; each vertex has 4 to 32 live slots. A slot at or above 512 names peer p and position k with k below send_counts of that peer for this device. Hub indices are skewed: some hubs are read far more than others. `hub_slots`: the 1 entries of one device are distinct local rows. `send_rows`: rows may repeat; entries at or past a peer's count are not live. `send_counts`: in every partition group one shard index receives 4 rows from every peer.
All inputs are finite; a program needn't handle non-finite values.
Results may differ from a plain program's by a relative error of at most 0.0052.
Values may be sent and summed in bfloat16 or wider, within the bound.
No kernel may reach another device: no remote copies, remote signals or barrier semaphores. Data moves between devices by JAX's collectives and lax.ppermute only.
A program may use at most 64 MiB of HBM per device.

v0:
```python
import jax
import jax.numpy as jnp
from jax import lax
from jax.sharding import PartitionSpec as P

row_block = 128


def contract_rows(left, right):
    return lax.dot_general(
        left, right, (((0,), (0,)), ((), ())), preferred_element_type=jnp.float32
    )


def contract_cols(left, right):
    return lax.dot_general(
        left, right, (((1,), (1,)), ((), ())), preferred_element_type=jnp.float32
    )


def body(features, w_self, w_neigh, cotangent, neighbours, hub_slots, send_rows, send_counts):
    verts, width = features.shape
    slots = neighbours.shape[1]
    peers = lax.axis_size("shard")
    routes = send_rows[0]
    counts = send_counts[0]
    cap = routes.shape[1]
    live = jnp.arange(cap)[None, :] < counts[:, None]
    hub_local = features[hub_slots]
    hubs = lax.all_gather(hub_local, ("dom", "shard"), axis=0, tiled=True)
    outgoing = jnp.where(live[:, :, None], features[routes], jnp.zeros((), jnp.bfloat16))
    incoming = lax.all_to_all(outgoing, "shard", split_axis=0, concat_axis=0, tiled=True)
    hub_count = hubs.shape[0]
    table_size = verts + hub_count + peers * cap
    table = jnp.concatenate(
        [features, hubs, incoming.reshape(peers * cap, width), jnp.zeros((1, width), jnp.bfloat16)],
        axis=0,
    )
    degree = jnp.sum(neighbours < table_size, axis=1).astype(jnp.float32)
    blocks = neighbours.reshape(verts // row_block, row_block, slots)
    sums = lax.map(lambda blk: jnp.sum(table[blk], axis=1, dtype=jnp.float32), blocks).reshape(
        verts, width
    )
    agg = (sums / degree[:, None]).astype(jnp.bfloat16)
    z = jnp.dot(features, w_self, preferred_element_type=jnp.float32) + jnp.dot(
        agg, w_neigh, preferred_element_type=jnp.float32
    )
    sig = jax.nn.sigmoid(z)
    hidden = (z * sig).astype(jnp.bfloat16)
    dz = (cotangent.astype(jnp.float32) * sig * (1.0 + z * (1.0 - sig))).astype(jnp.bfloat16)
    grad_self, grad_neigh = lax.psum(
        (contract_rows(features, dz), contract_rows(agg, dz)), ("dom", "shard")
    )
    edge_grad = contract_cols(dz, w_neigh) / degree[:, None]
    grads = edge_grad.reshape(verts // row_block, row_block, width)

    def add_block(acc, pair):
        blk, grad = pair
        spread = jnp.broadcast_to(grad[:, None, :], (row_block, slots, width)).reshape(-1, width)
        return (acc.at[blk.reshape(-1)].add(spread), None)

    start = jnp.zeros((table_size + 1, width), jnp.float32)
    accum, _ = lax.scan(add_block, start, (blocks, grads))
    hub_part = accum[verts : verts + hub_count]
    hub_back = lax.psum_scatter(hub_part, ("dom", "shard"), scatter_dimension=0, tiled=True)
    recv_part = accum[verts + hub_count : table_size].reshape(peers, cap, width)
    returned = lax.all_to_all(
        recv_part.astype(jnp.bfloat16), "shard", split_axis=0, concat_axis=0, tiled=True
    ).astype(recv_part.dtype)
    returned = jnp.where(live[:, :, None], returned, 0.0)
    grad_features = contract_cols(dz, w_self) + accum[:verts]
    grad_features = grad_features.at[hub_slots].add(hub_back)
    grad_features = grad_features.at[routes.reshape(-1)].add(returned.reshape(-1, width))
    return (hidden, grad_features, grad_self, grad_neigh)


def solution(mesh):
    return jax.shard_map(
        body,
        mesh=mesh,
        in_specs=(
            P(("dom", "shard"), None),
            P(),
            P(),
            P(("dom", "shard"), None),
            P(("dom", "shard"), None),
            P(("dom", "shard")),
            P(("dom", "shard"), None, None),
            P(("dom", "shard"), None),
        ),
        out_specs=(P(("dom", "shard"), None), P(("dom", "shard"), None), P(), P()),
        check_vma=False,
    )
```

profile of v0, /device:TPU:8, one launch (start us, length us, event | category | flops | bytes accessed | tf_op | source)
XLA Modules:
  0.0 480.2 jit_solution(18046370803552838058)
XLA Ops:
  8.2 1.9 gather_fusion.1
  11.0 11.3 %all-to-all-start = ((bf16[32,4,512]{2,1,0:T(4,128)(2,1)}), bf16[32,4,512]{2,1,0:T(4,128)(2,1)S(1)}, u32[]{:S(2)}, u32[]{:S(2)}) async-start(bf16[32,4,512]{2,1,0:T(4,128)(2,1)} %broadcast_select_fusion), calls=%async_computation | async-start | bytes 262144 | tf_op jit(solution)/shard_map/all_to_all | solution.py:32
  23.2 69.5 %all-gather = bf16[256,1,512]{2,1,0:T(2,128)(2,1)S(1)} all-gather(bf16[1,1,512]{2,1,0:T(2,128)(2,1)S(1)} %dynamic-slice_bitcast_fusion.1), channel_id=1, replica_groups=mesh['dom'=8,'shard'=32] {'dom','shard'}, dimensions={0}, use_global_device_ids=true | all-gather | bytes 263168 | tf_op jit(solution)/shard_map/all_gather | solution.py:30
  93.4 42.3 %while.22 = (s32[]{:T(128)}, f32[2,128,512]{2,1,0:T(8,128)S(1)}, s32[2,128,32]{2,1,0:T(8,128)S(1)}, bf16[641,512]{1,0:T(8,128)(2,1)S(1)}, s32[]{:T(128)}) while((s32[]{:T(128)}, f32[2,128,512]{2,1,0:T(8,128)S(1)}, s32[2,128,32]{2,1,0:T(8,128)S(1)}, bf16[641,512]{1,0:T(8,128)(2,1)S(1)}, s32[]{:T(128)}) %tuple.59), condition=%wide.region_2.3_spmd, body=%wide.region_0.0_spmd.sunk | while | flops 4145154 | bytes 13484109 | solution.py:41
  93.5 17.3 %gather_fusion = bf16[4096,512]{1,0:T(8,128)(2,1)} fusion(bf16[641,512]{1,0:T(8,128)(2,1)S(1)} %get-tuple-element.173, s32[4096]{0:T(1024)S(1)} %broadcast_clamp_fusion.2), kind=kCustom, calls=%fused_computation.clone.1 | custom fusion | bytes 8404992 | tf_op jit(solution)/shard_map/while/body/eval_jaxpr/gather | solution.py:41
  110.8 3.7 convert_reduce_fusion.3
  114.6 17.3 %gather_fusion = bf16[4096,512]{1,0:T(8,128)(2,1)} fusion(bf16[641,512]{1,0:T(8,128)(2,1)S(1)} %get-tuple-element.173, s32[4096]{0:T(1024)S(1)} %broadcast_clamp_fusion.2), kind=kCustom, calls=%fused_computation.clone.1 | custom fusion | bytes 8404992 | tf_op jit(solution)/shard_map/while/body/eval_jaxpr/gather | solution.py:41
  132.0 3.7 convert_reduce_fusion.3
  135.8 1.2 multiply_convert_fusion
  137.4 1.3 convolution_bitcast_fusion
  138.7 1.3 fusion.3
  140.1 61.5 %while.23 = (s32[]{:T(128)}, f32[641,512]{1,0:T(8,128)S(1)}, s32[2,128,32]{2,1,0:T(8,128)S(1)}, f32[2,128,512]{2,1,0:T(8,128)S(1)}, s32[]{:T(128)}) while((s32[]{:T(128)}, f32[641,512]{1,0:T(8,128)S(1)}, s32[2,128,32]{2,1,0:T(8,128)S(1)}, f32[2,128,512]{2,1,0:T(8,128)S(1)}, s32[]{:T(128)}) %tuple.61), condition=%wide.region_6.7_spmd, body=%wide.region_4.6_spmd.sunk | while | flops 2109442 | bytes 34455628 | solution.py:63
  140.3 4.3 broadcast_in_dim.68
  144.6 26.2 %scatter_fusion = f32[641,512]{1,0:T(8,128)S(1)} fusion(f32[641,512]{1,0:T(8,128)S(1)} %get-tuple-element.181, s32[4096]{0:T(1024)S(1)} %bitcast.62, f32[4096,512]{1,0:T(8,128)} %bitcast.59), kind=kCustom, calls=%fused_computation.2.clone.1 | custom fusion | flops 2097152 | bytes 25182208 | tf_op jit(solution)/shard_map/while/body/eval_jaxpr/scatter-add | solution.py:60
  171.0 4.3 broadcast_in_dim.68
  175.3 26.3 %scatter_fusion = f32[641,512]{1,0:T(8,128)S(1)} fusion(f32[641,512]{1,0:T(8,128)S(1)} %get-tuple-element.181, s32[4096]{0:T(1024)S(1)} %bitcast.62, f32[4096,512]{1,0:T(8,128)} %bitcast.59), kind=kCustom, calls=%fused_computation.2.clone.1 | custom fusion | flops 2097152 | bytes 25182208 | tf_op jit(solution)/shard_map/while/body/eval_jaxpr/scatter-add | solution.py:60
  201.6 0.8 slice.25
  204.8 7.0 %all-to-all-start.1 = ((bf16[32,4,512]{2,1,0:T(4,128)(2,1)}), bf16[32,4,512]{2,1,0:T(4,128)(2,1)S(1)}, u32[]{:S(2)}, u32[]{:S(2)}) async-start(bf16[32,4,512]{2,1,0:T(4,128)(2,1)} %convert_element_type.38), calls=%async_computation.1 | async-start | bytes 262144 | tf_op jit(solution)/shard_map/all_to_all | solution.py:67
  212.2 10.3 %all-to-all-done.1 = bf16[32,4,512]{2,1,0:T(4,128)(2,1)S(1)} async-done(((bf16[32,4,512]{2,1,0:T(4,128)(2,1)}), bf16[32,4,512]{2,1,0:T(4,128)(2,1)S(1)}, u32[]{:S(2)}, u32[]{:S(2)}) %all-to-all-start.1) | async-done | bytes 131104 | tf_op jit(solution)/shard_map/all_to_all | solution.py:67
  222.7 244.0 %all-reduce.4.cloned.1.call-done = (f32[256,512]{1,0:T(8,128)}, f32[512,512]{0,1:T(8,128)}, f32[512,512]{1,0:T(8,128)}) async-done(((f32[256,512]{1,0:T(8,128)}, f32[512,512]{0,1:T(8,128)}, f32[512,512]{1,0:T(8,128)}), (f32[256,512]{1,0:T(8,128)}, f32[512,512]{0,1:T(8,128)}, f32[512,512]{1,0:T(8,128)})) %all-reduce.4.cloned.1.call-update) | async-done | bytes 2621456
  466.7 1.3 broadcast_select_fusion.1
  468.1 2.5 copy.27
  470.7 1.5 scatter_fusion.1
  472.2 1.0 copy.51
  (79 shorter events, 6.8 us)
Async XLA Ops:
  7.2 128.6 %copy-start = (bf16[512,512]{1,0:T(8,128)(2,1)S(1)}, bf16[512,512]{1,0:T(8,128)(2,1)}, u32[]{:S(2)}) copy-start(bf16[512,512]{1,0:T(8,128)(2,1)} %param.16) | copy-start | bytes 1572868
  7.2 16.0 %copy-start.2 = (bf16[256,512]{1,0:T(8,128)(2,1)S(1)}, bf16[256,512]{1,0:T(8,128)(2,1)}, u32[]{:S(2)}) copy-start(bf16[256,512]{1,0:T(8,128)(2,1)} %param.14) | copy-start | bytes 786436
  7.2 2.9 copy-start.12
  7.2 15.2 %copy-start.8 = (s32[256,32]{0,1:T(8,128)S(1)}, s32[256,32]{0,1:T(8,128)}, u32[]{:S(2)}) copy-start(s32[256,32]{0,1:T(8,128)} %param.18) | copy-start | bytes 98308
  10.0 82.7 %copy-start.5 = (bf16[512,512]{1,0:T(8,128)(2,1)S(1)}, bf16[512,512]{1,0:T(8,128)(2,1)}, u32[]{:S(2)}) copy-start(bf16[512,512]{1,0:T(8,128)(2,1)} %param.15) | copy-start | bytes 1572868
  10.2 0.8 copy-start.9
  11.0 82.1 %all-to-all-start = ((bf16[32,4,512]{2,1,0:T(4,128)(2,1)}), bf16[32,4,512]{2,1,0:T(4,128)(2,1)S(1)}, u32[]{:S(2)}, u32[]{:S(2)}) async-start(bf16[32,4,512]{2,1,0:T(4,128)(2,1)} %broadcast_select_fusion), calls=%async_computation | async-start | bytes 262144 | tf_op jit(solution)/shard_map/all_to_all | solution.py:32
  22.3 444.4 %all-reduce.4.cloned.1.call-start = ((), (), s32[]{:S(2)}) async-start(), calls=%async_computation.2 | async-start | bytes 5242880
  93.3 42.5 %copy-start.14 = (bf16[256,512]{1,0:T(8,128)(2,1)S(1)}, bf16[256,512]{1,0:T(8,128)(2,1)}, u32[]{:S(2)}) copy-start(bf16[256,512]{1,0:T(8,128)(2,1)} %param.17) | copy-start | bytes 786436
  137.0 1.6 copy-start.3
  202.5 0.7 copy-start.11
  202.5 0.9 copy-start.13
  202.5 9.4 %copy-start.4 = (bf16[256,512]{1,0:T(8,128)(2,1)S(1)}, bf16[256,512]{1,0:T(8,128)(2,1)}, u32[]{:S(2)}) copy-start(bf16[256,512]{1,0:T(8,128)(2,1)} %copy-done.3) | copy-start | bytes 786436
  202.5 9.4 %copy-start.6 = (bf16[512,512]{1,0:T(8,128)(2,1)S(1)}, bf16[512,512]{1,0:T(8,128)(2,1)}, u32[]{:S(2)}) copy-start(bf16[512,512]{1,0:T(8,128)(2,1)} %param.15) | copy-start | bytes 1572868
  203.2 19.3 %copy-start.10 = (pred[32,4]{1,0:T(8,128)(4,1)S(1)}, pred[32,4]{1,0:T(8,128)(4,1)}, u32[]{:S(2)}) copy-start(pred[32,4]{1,0:T(8,128)(4,1)} %copy-done.9) | copy-start | bytes 388
  204.8 17.6 %all-to-all-start.1 = ((bf16[32,4,512]{2,1,0:T(4,128)(2,1)}), bf16[32,4,512]{2,1,0:T(4,128)(2,1)S(1)}, u32[]{:S(2)}, u32[]{:S(2)}) async-start(bf16[32,4,512]{2,1,0:T(4,128)(2,1)} %convert_element_type.38), calls=%async_computation.1 | async-start | bytes 262144 | tf_op jit(solution)/shard_map/all_to_all | solution.py:67
  470.7 1.6 copy-start.7
  472.2 1.1 copy-start.1
Sparse Core Ops, SparseCore 0:
  202.6 264.0 all-reduce.3
where the time goes:
time: 481 us; the launch traced here: 480 us
  waiting for transfers between devices  254 us (53%)
  blocking collectives  69.5 us (14%)
  other arithmetic  65.7 us (14%)
  local copies, waits for them, and re-layouts  52.4 us (11%)
  starting transfers between devices  18.3 us (4%)
  between operations  15 us (3%)
    unnamed x2, waiting for transfers between devices  244 us
    all_gather x1, blocking collectives, body(): hubs = lax.all_gather(hub_local, ('dom', 'shard'), axis=0, tiled=True)  69.5 us
    scatter-add x2, other arithmetic, add_block(): return (acc.at[blk.reshape(-1)].add(spread), None)  52.5 us
    gather x2, local copies, waits for them, and re-layouts, body(): table[blk]  34.6 us
    all_to_all x1, starting transfers between devices, body(): lax.all_to_all(outgoing, 'shard', split_axis=0, concat_axis=0, tiled=True)  11.3 us
    all_to_all x1, waiting for transfers between devices, body(): lax.all_to_all(recv_part.astype(jnp.bfloat16), 'shard', split_axis=0, con...  10.3 us
  transfers between devices with their start and end apart: 3, of which 2 were waited for; matrix products, arithmetic and copies ran while one was open for 1% of the time, Pallas kernels for 0%

commit v1 on v0

--- a/solution.py
+++ b/solution.py
@@ -2,6 +2,7 @@
 import jax.numpy as jnp
 from jax import lax
 from jax.sharding import PartitionSpec as P
+from jax.lax import all_to_all, axis_size
 
 row_block = 128
 
@@ -27,7 +28,15 @@
     cap = routes.shape[1]
     live = jnp.arange(cap)[None, :] < counts[:, None]
     hub_local = features[hub_slots]
-    hubs = lax.all_gather(hub_local, ("dom", "shard"), axis=0, tiled=True)
+    hubs = jnp.concatenate(
+        all_to_all(
+            jnp.stack([hub_local for _ in range(axis_size(("dom", "shard")))], axis=0),
+            axis_name=("dom", "shard"),
+            split_axis=0,
+            concat_axis=0,
+        ),
+        axis=0,
+    )
     outgoing = jnp.where(live[:, :, None], features[routes], jnp.zeros((), jnp.bfloat16))
     incoming = lax.all_to_all(outgoing, "shard", split_axis=0, concat_axis=0, tiled=True)
     hub_count = hubs.shape[0]

time: 481 us -> 437 us (0.909)
  blocking collectives: 69.5 us -> 0 us
  waiting for transfers between devices: 254 us -> 272 us
    all_gather x1 -> x0, blocking collectives: 69.5 us -> none  [body(): hubs = lax.all_gather(hub_local, ('dom', 'shard'), axis=0, tiled=True)]
    all_to_all x0 -> x1, waiting for transfers between devices: none -> 14.2 us  [body(): all_to_all(jnp.stack([hub_local for _ in range(axis_size(('dom', 'shard')...]
    all_to_all x0 -> x1, starting transfers between devices: none -> 7.4 us  [body(): all_to_all(jnp.stack([hub_local for _ in range(axis_size(('dom', 'shard')...]
    all_to_all x1, waiting for transfers between devices: 0.01 us -> 5.68 us  [body(): lax.all_to_all(outgoing, 'shard', split_axis=0, concat_axis=0, tiled=True)]
  transfers between devices with their start and end apart: 3 -> 4, of which waited for: 2 -> 4; matrix products, arithmetic and copies ran while one was open for 1% -> 1% of each run, Pallas kernels for 0% -> 0%
where the time goes in v1:
time: 437 us
  waiting for transfers between devices  272 us (62%)
  other arithmetic  67.8 us (16%)
  local copies, waits for them, and re-layouts  54.1 us (12%)
  starting transfers between devices  22.7 us (5%)
  between operations  15.1 us (3%)
  matrix products  4.76 us (1%)
    unnamed x2, waiting for transfers between devices  242 us
    scatter-add x2, other arithmetic, add_block(): return (acc.at[blk.reshape(-1)].add(spread), None)  52.5 us
    gather x2, local copies, waits for them, and re-layouts, body(): table[blk]  34.5 us
    all_to_all x1, waiting for transfers between devices, body(): all_to_all(jnp.stack([hub_local for _ in range(axis_size(('dom', 'shard')...  14.2 us
    all_to_all x1, starting transfers between devices, body(): lax.all_to_all(outgoing, 'shard', split_axis=0, concat_axis=0, tiled=True)  11.4 us
    all_to_all x1, waiting for transfers between devices, body(): lax.all_to_all(recv_part.astype(jnp.bfloat16), 'shard', split_axis=0, con...  10.5 us
  transfers between devices with their start and end apart: 4, of which 4 were waited for; matrix products, arithmetic and copies ran while one was open for 1% of the time, Pallas kernels for 0%

profile of v1, /device:TPU:8, one launch (start us, length us, event | category | flops | bytes accessed | tf_op | source)
XLA Modules:
  0.0 436.9 jit_solution(1074457856630310040)
XLA Ops:
  8.2 1.9 gather_fusion.1
  11.0 11.4 %all-to-all-start.1 = ((bf16[32,4,512]{2,1,0:T(4,128)(2,1)}), bf16[32,4,512]{2,1,0:T(4,128)(2,1)S(1)}, u32[]{:S(2)}, u32[]{:S(2)}) async-start(bf16[32,4,512]{2,1,0:T(4,128)(2,1)} %broadcast_select_fusion), calls=%async_computation.1 | async-start | bytes 262144 | tf_op jit(solution)/shard_map/all_to_all | solution.py:41
  24.0 2.3 reduce.10
  27.0 5.7 %all-to-all-done.1 = bf16[32,4,512]{2,1,0:T(4,128)(2,1)S(1)} async-done(((bf16[32,4,512]{2,1,0:T(4,128)(2,1)}), bf16[32,4,512]{2,1,0:T(4,128)(2,1)S(1)}, u32[]{:S(2)}, u32[]{:S(2)}) %all-to-all-start.1) | async-done | bytes 131104 | tf_op jit(solution)/shard_map/all_to_all | solution.py:41
  32.7 7.4 %all-to-all-start = ((bf16[256,2,256]{2,1,0:T(2,128)(2,1)}), bf16[256,2,256]{2,1,0:T(2,128)(2,1)S(1)}, u32[]{:S(2)}, u32[]{:S(2)}) async-start(bf16[256,2,256]{2,1,0:T(2,128)(2,1)} %reshape.270), calls=%async_computation | async-start | bytes 524288 | tf_op jit(solution)/shard_map/all_to_all | solution.py:32
  40.7 14.2 %all-to-all-done = bf16[256,2,256]{2,1,0:T(2,128)(2,1)S(1)} async-done(((bf16[256,2,256]{2,1,0:T(2,128)(2,1)}), bf16[256,2,256]{2,1,0:T(2,128)(2,1)S(1)}, u32[]{:S(2)}, u32[]{:S(2)}) %all-to-all-start) | async-done | bytes 262176 | tf_op jit(solution)/shard_map/all_to_all | solution.py:32
  55.3 42.2 %while.22 = (s32[]{:T(128)}, f32[2,128,512]{2,1,0:T(8,128)S(1)}, s32[2,128,32]{2,1,0:T(8,128)S(1)}, bf16[641,512]{1,0:T(8,128)(2,1)S(1)}, s32[]{:T(128)}) while((s32[]{:T(128)}, f32[2,128,512]{2,1,0:T(8,128)S(1)}, s32[2,128,32]{2,1,0:T(8,128)S(1)}, bf16[641,512]{1,0:T(8,128)(2,1)S(1)}, s32[]{:T(128)}) %tuple.59), condition=%wide.region_2.3_spmd, body=%wide.region_0.0_spmd.sunk | while | flops 4145154 | bytes 13484109 | solution.py:50
  55.5 17.3 %gather_fusion = bf16[4096,512]{1,0:T(8,128)(2,1)} fusion(bf16[641,512]{1,0:T(8,128)(2,1)S(1)} %get-tuple-element.173, s32[4096]{0:T(1024)S(1)} %broadcast_clamp_fusion.2), kind=kCustom, calls=%fused_computation.clone.1 | custom fusion | bytes 8404992 | tf_op jit(solution)/shard_map/while/body/eval_jaxpr/gather | solution.py:50
  72.7 3.7 convert_reduce_fusion.3
  76.6 17.3 %gather_fusion = bf16[4096,512]{1,0:T(8,128)(2,1)} fusion(bf16[641,512]{1,0:T(8,128)(2,1)S(1)} %get-tuple-element.173, s32[4096]{0:T(1024)S(1)} %broadcast_clamp_fusion.2), kind=kCustom, calls=%fused_computation.clone.1 | custom fusion | bytes 8404992 | tf_op jit(solution)/shard_map/while/body/eval_jaxpr/gather | solution.py:50
  93.9 3.7 convert_reduce_fusion.3
  99.3 1.3 convolution_bitcast_fusion
  100.6 1.3 fusion.3
  102.0 61.5 %while.23 = (s32[]{:T(128)}, f32[641,512]{1,0:T(8,128)S(1)}, s32[2,128,32]{2,1,0:T(8,128)S(1)}, f32[2,128,512]{2,1,0:T(8,128)S(1)}, s32[]{:T(128)}) while((s32[]{:T(128)}, f32[641,512]{1,0:T(8,128)S(1)}, s32[2,128,32]{2,1,0:T(8,128)S(1)}, f32[2,128,512]{2,1,0:T(8,128)S(1)}, s32[]{:T(128)}) %tuple.61), condition=%wide.region_6.7_spmd, body=%wide.region_4.6_spmd.sunk | while | flops 2109442 | bytes 34455628 | solution.py:72
  102.2 4.3 broadcast_in_dim.68
  106.5 26.2 %scatter_fusion = f32[641,512]{1,0:T(8,128)S(1)} fusion(f32[641,512]{1,0:T(8,128)S(1)} %get-tuple-element.181, s32[4096]{0:T(1024)S(1)} %bitcast.60, f32[4096,512]{1,0:T(8,128)} %bitcast.57), kind=kCustom, calls=%fused_computation.2.clone.1 | custom fusion | flops 2097152 | bytes 25182208 | tf_op jit(solution)/shard_map/while/body/eval_jaxpr/scatter-add | solution.py:69
  132.9 4.3 broadcast_in_dim.68
  137.2 26.3 %scatter_fusion = f32[641,512]{1,0:T(8,128)S(1)} fusion(f32[641,512]{1,0:T(8,128)S(1)} %get-tuple-element.181, s32[4096]{0:T(1024)S(1)} %bitcast.60, f32[4096,512]{1,0:T(8,128)} %bitcast.57), kind=kCustom, calls=%fused_computation.2.clone.1 | custom fusion | flops 2097152 | bytes 25182208 | tf_op jit(solution)/shard_map/while/body/eval_jaxpr/scatter-add | solution.py:69
  166.6 3.9 all-to-all-start.2
  170.9 10.5 %all-to-all-done.2 = bf16[32,4,512]{2,1,0:T(4,128)(2,1)S(1)} async-done(((bf16[32,4,512]{2,1,0:T(4,128)(2,1)}), bf16[32,4,512]{2,1,0:T(4,128)(2,1)S(1)}, u32[]{:S(2)}, u32[]{:S(2)}) %all-to-all-start.2) | async-done | bytes 131104 | tf_op jit(solution)/shard_map/all_to_all | solution.py:76
  181.6 241.9 %all-reduce.4.cloned.1.call-done = (f32[256,512]{1,0:T(8,128)}, f32[512,512]{0,1:T(8,128)}, f32[512,512]{1,0:T(8,128)}) async-done(((f32[256,512]{1,0:T(8,128)}, f32[512,512]{0,1:T(8,128)}, f32[512,512]{1,0:T(8,128)}), (f32[256,512]{1,0:T(8,128)}, f32[512,512]{0,1:T(8,128)}, f32[512,512]{1,0:T(8,128)})) %all-reduce.4.cloned.1.call-update) | async-done | bytes 2621456
  423.5 1.3 broadcast_select_fusion.1
  424.8 2.5 copy.27
  427.3 1.5 scatter_fusion.1
  (85 shorter events, 11.6 us)
Async XLA Ops:
  7.2 90.5 %copy-start = (bf16[512,512]{1,0:T(8,128)(2,1)S(1)}, bf16[512,512]{1,0:T(8,128)(2,1)}, u32[]{:S(2)}) copy-start(bf16[512,512]{1,0:T(8,128)(2,1)} %param.16) | copy-start | bytes 1572868
  7.2 16.0 %copy-start.2 = (bf16[256,512]{1,0:T(8,128)(2,1)S(1)}, bf16[256,512]{1,0:T(8,128)(2,1)}, u32[]{:S(2)}) copy-start(bf16[256,512]{1,0:T(8,128)(2,1)} %param.14) | copy-start | bytes 786436
  7.2 2.9 copy-start.12
  10.2 0.8 copy-start.9
  11.0 29.2 %copy-start.8 = (s32[256,32]{0,1:T(8,128)S(1)}, s32[256,32]{0,1:T(8,128)}, u32[]{:S(2)}) copy-start(s32[256,32]{0,1:T(8,128)} %param.18) | copy-start | bytes 98308
  11.0 21.7 %all-to-all-start.1 = ((bf16[32,4,512]{2,1,0:T(4,128)(2,1)}), bf16[32,4,512]{2,1,0:T(4,128)(2,1)S(1)}, u32[]{:S(2)}, u32[]{:S(2)}) async-start(bf16[32,4,512]{2,1,0:T(4,128)(2,1)} %broadcast_select_fusion), calls=%async_computation.1 | async-start | bytes 262144 | tf_op jit(solution)/shard_map/all_to_all | solution.py:41
  22.4 17.9 %copy-start.5 = (bf16[512,512]{1,0:T(8,128)(2,1)S(1)}, bf16[512,512]{1,0:T(8,128)(2,1)}, u32[]{:S(2)}) copy-start(bf16[512,512]{1,0:T(8,128)(2,1)} %param.15) | copy-start | bytes 1572868
  32.7 22.2 %all-to-all-start = ((bf16[256,2,256]{2,1,0:T(2,128)(2,1)}), bf16[256,2,256]{2,1,0:T(2,128)(2,1)S(1)}, u32[]{:S(2)}, u32[]{:S(2)}) async-start(bf16[256,2,256]{2,1,0:T(2,128)(2,1)} %reshape.270), calls=%async_computation | async-start | bytes 524288 | tf_op jit(solution)/shard_map/all_to_all | solution.py:32
  40.1 383.4 %all-reduce.4.cloned.1.call-start = ((), (), s32[]{:S(2)}) async-start(), calls=%async_computation.3 | async-start | bytes 5242880
  55.3 42.4 %copy-start.14 = (bf16[256,512]{1,0:T(8,128)(2,1)S(1)}, bf16[256,512]{1,0:T(8,128)(2,1)}, u32[]{:S(2)}) copy-start(bf16[256,512]{1,0:T(8,128)(2,1)} %param.17) | copy-start | bytes 786436
  98.9 1.6 copy-start.3
  164.4 0.7 copy-start.11
  164.4 0.9 copy-start.13
  164.4 6.1 %copy-start.4 = (bf16[256,512]{1,0:T(8,128)(2,1)S(1)}, bf16[256,512]{1,0:T(8,128)(2,1)}, u32[]{:S(2)}) copy-start(bf16[256,512]{1,0:T(8,128)(2,1)} %copy-done.3) | copy-start | bytes 786436
  164.4 6.2 %copy-start.6 = (bf16[512,512]{1,0:T(8,128)(2,1)S(1)}, bf16[512,512]{1,0:T(8,128)(2,1)}, u32[]{:S(2)}) copy-start(bf16[512,512]{1,0:T(8,128)(2,1)} %param.15) | copy-start | bytes 1572868
  165.1 16.2 %copy-start.10 = (pred[32,4]{1,0:T(8,128)(4,1)S(1)}, pred[32,4]{1,0:T(8,128)(4,1)}, u32[]{:S(2)}) copy-start(pred[32,4]{1,0:T(8,128)(4,1)} %copy-done.9) | copy-start | bytes 388
  166.6 14.7 %all-to-all-start.2 = ((bf16[32,4,512]{2,1,0:T(4,128)(2,1)}), bf16[32,4,512]{2,1,0:T(4,128)(2,1)S(1)}, u32[]{:S(2)}, u32[]{:S(2)}) async-start(bf16[32,4,512]{2,1,0:T(4,128)(2,1)} %convert_element_type.38), calls=%async_computation.2 | async-start | bytes 262144 | tf_op jit(solution)/shard_map/all_to_all | solution.py:76
  427.3 1.6 copy-start.7
  428.9 1.1 copy-start.1
Sparse Core Ops, SparseCore 0:
  164.5 258.9 all-reduce.3
